TPU v7x, 512 devices: a whole 4x8x8 slice. The times are simulated.
512 devices in a mesh: row: 16 (over z, y_lo), col: 8 (over y_hi, core), rep: 4 (over x).
Axes of the slice: x: 4, y: 8 (y_hi: 4, y_lo: 2; y = y_hi * 2 + y_lo), z: 8, core: 2. Of those that a mesh axis runs over, the one named last changes fastest.
Arguments:
- genotypes: bfloat16 [2048, 16384], P(('row', 'col', 'rep')), may hold values from 0 to 2, as said below
Outputs:
- main_tiles: float32 [16, 8, 1024, 1024], P('row', 'col', 'rep')
- half_tiles: float32 [16, 1024, 1024], P('row', 'rep', 'col')
Inputs may be any that keep to these rules, and one draw needn't show every extreme that they name: `genotypes`: imputed dosages of the alternate allele, real-valued.
All inputs are finite; a program needn't handle non-finite values.
Results may differ from a plain program's by a relative error of at most 0.008.
Values may be sent and summed in bfloat16 or wider, within the bound.
No kernel may reach another device: no remote copies, remote signals or barrier semaphores. Data moves between devices by JAX's collectives and lax.ppermute only.
A program may use at most 64 MiB of HBM per device.

v0:
```python
import functools

import jax
import jax.numpy as jnp
from jax import lax
from jax.experimental import pallas as pl
from jax.experimental.pallas import tpu as pltpu
from jax.sharding import PartitionSpec as P


F32 = jnp.float32
BF16 = jnp.bfloat16
EPS = 1e-05


def params(mib):
    return pltpu.CompilerParams(vmem_limit_bytes=mib << 20)


def cost(flops, size):
    return pl.CostEstimate(flops=flops, bytes_accessed=size, transcendentals=0)


def thirds(v):
    hi = v.astype(BF16).astype(F32)
    rest = v - hi
    mid = rest.astype(BF16).astype(F32)
    return hi, mid, (rest - mid).astype(BF16).astype(F32)


def sums(v):
    v = v.astype(F32)
    return jnp.sum(v, axis=0, keepdims=True), jnp.sum(v * v, axis=0, keepdims=True)


def stacked(rows, count, held=None):
    gap = jnp.zeros((count - (held or len(rows)), rows[0].shape[1]), F32)
    return jnp.concatenate([*rows, gap], axis=0)


def dot0(a, b):
    return lax.dot_general(a, b, (((0,), (0,)), ((), ())), preferred_element_type=F32)


def pack_body(n_row, n_col, x_ref, out_ref):
    width = x_ref.shape[1] // n_row
    half, slab = width // 2, width // n_col
    for r in range(n_row):
        for c in range(n_col):
            d = r * n_col + c
            near = r * width + (c % 2) * half
            pair = ((r + c) % n_row) * width + (c % 2) * half
            far = ((r + n_row // 2) % n_row) * width + c * slab
            out_ref[d, :, :half] = x_ref[:, near : near + half]
            out_ref[d, :, half : 2 * half] = x_ref[:, pair : pair + half]
            out_ref[d, :, 2 * half :] = x_ref[:, far : far + slab]


def split_body(in_ref, pair_ref, core_ref, own_ref):
    half = pair_ref.shape[2]
    core_ref[...] = in_ref[:, :, :half]
    pair_ref[...] = in_ref[:, :, half : 2 * half]
    own_ref[...] = in_ref[...].reshape(own_ref.shape)


def column_side(right):
    samples = right.shape[0]
    dose, square = sums(right)
    hi, mid, lo = thirds(dose)
    fix = (stacked([hi, mid, hi, mid, lo, hi], 8) * (-1.0 / samples)).astype(BF16)
    mean = dose / samples
    return fix, [*thirds(mean), *thirds(square - dose * mean)]


def partners(group):
    return group, group + 1 - 2 * lax.rem(group, 2), 3 - group, lax.rem(group + 2, 4)


def piece(q, left_ref, right, right_fix, foot, out_ref):
    rows, cols = out_ref.shape
    sub, samples = rows - 16, left_ref.shape[0]
    left = left_ref[:, pl.ds(pl.multiple_of(q * sub, sub), sub)]
    dose, square = sums(left)
    hi, mid, lo = thirds(dose)
    left_fix = stacked([hi, hi, mid, mid, hi, lo], 8).astype(BF16)
    mean = dose / samples
    gap = jnp.zeros((1, cols - sub), F32)
    mine = [*thirds(mean), *thirds(square - dose * mean)]
    mine = [jnp.concatenate([v, gap], axis=1) for v in mine]
    part = dot0(left, right) + dot0(left_fix, right_fix)
    out_ref[:sub, :] = part.astype(BF16)
    out_ref[sub:, :] = stacked([foot[:6], *mine], 16, 12).astype(BF16)
    return left_fix


def tile_across(own_ref, other_ref, left_ref, fix_ref, right_fix_ref, foot_ref, out_ref):
    samples, half = own_ref.shape[0], other_ref.shape[2]
    core = lax.rem(lax.axis_index("col"), 2)
    left_ref[:, pl.ds(pl.multiple_of(core * half, half), half)] = own_ref[:, :half]
    left_ref[:, pl.ds(pl.multiple_of((1 - core) * half, half), half)] = other_ref[...].reshape(samples, half)
    right = own_ref[:, half:]
    right_fix, col_rows = column_side(right)
    foot = stacked(col_rows, 8)
    right_fix_ref[...] = right_fix
    foot_ref[...] = foot
    q = partners(lax.axis_index("rep"))[3]
    fix_ref[...] = piece(q, left_ref, right, right_fix, foot, out_ref)


def tile_others(left_ref, across_ref, right_fix_ref, foot_ref, own_ref, fix_ref, *out_refs):
    sub, half = across_ref.shape[1], left_ref.shape[1] // 2
    *near, opposite = partners(lax.axis_index("rep"))
    fix_ref[:, pl.ds(pl.multiple_of(opposite * sub, sub), sub)] = across_ref[...]
    right, right_fix, foot = own_ref[:, half:], right_fix_ref[...], foot_ref[...]
    for q, ref in zip((near[1], near[2], near[0]), (out_refs[1], out_refs[2], out_refs[0])):
        fix_ref[:, pl.ds(pl.multiple_of(q * sub, sub), sub)] = piece(q, left_ref, right, right_fix, foot, ref)


def tile_second(left_ref, fix_ref, swapped_ref, out_ref, held_ref, sems):
    n_rep, rows, cols = out_ref.shape
    sub, samples = rows - 8, left_ref.shape[0]
    right = swapped_ref[...].reshape(samples, cols)
    right_fix, col_rows = column_side(right)
    foot = stacked(col_rows, 8).astype(BF16)
    copies = []
    for q in range(n_rep):
        at = slice(q * sub, (q + 1) * sub)
        part = dot0(left_ref[:, at], right) + dot0(fix_ref[:, at], right_fix)
        held_ref[q, :sub, :] = part.astype(BF16)
        held_ref[q, sub:, :] = foot
        copies.append(pltpu.make_async_copy(held_ref.at[q], out_ref.at[q], sems.at[q]))
        copies[-1].start()
    for copy in copies:
        copy.wait()


def whole(means, squares, samples):
    count = len(means)
    mean = sum(means) / count
    off = [m - mean for m in means]
    spread = sum(squares) / (count * samples) + sum(o * o for o in off) / count
    return off, lax.rsqrt(spread + EPS)


def three(s, i):
    return s[i : i + 1] + s[i + 1 : i + 2] + s[i + 2 : i + 3]


def joined(parts, off, scale, turned, samples):
    n_rep = len(parts)
    total = sum(p.astype(F32) for p in parts)
    for q in range(n_rep):
        total += (turned[:, q : q + 1] * samples) * off[q]
    return total * turned[:, n_rep : n_rep + 1] * scale


def join_first(samples, *refs):
    *in_refs, turned_ref, main_ref, half_ref, near_ref, sem = refs
    sub, near = near_ref.shape
    n_rep = len(in_refs)
    stats = [r[sub:, :].astype(F32) for r in in_refs]
    l_off, l_scale = whole(
        [three(s[:, :sub], 6) for s in stats], [three(s[:, :sub], 9) for s in stats], samples
    )
    l_scale = l_scale / (n_rep * samples)
    turned = stacked(l_off + [l_scale], 8).T
    off, scale = whole([three(s, 0) for s in stats], [three(s, 3) for s in stats], samples)
    total = joined([r[:sub, :] for r in in_refs], off, scale, turned, samples)
    near_ref[...] = total[:, :near]
    core = lax.rem(lax.axis_index("col"), 2)
    to = pl.ds(pl.multiple_of(core * near, near), near)
    copy = pltpu.make_async_copy(near_ref, main_ref.at[:, to], sem)
    copy.start()
    half_ref[...] = total[:, near:]
    line = lax.broadcasted_iota(jnp.int32, (8, sub), 0)
    ordered = jnp.where(line == n_rep, l_scale, 0.0)
    for source, off in zip(partners(lax.axis_index("rep")), l_off):
        ordered = jnp.where(line == source, off, ordered)
    turned_ref[...] = ordered.T
    copy.wait()


def join_second(samples, in_ref, turned_ref, _, main_ref, held_ref, sems):
    n_rep, rows, half = in_ref.shape
    sub = rows - 8
    core = lax.rem(lax.axis_index("col"), 2)
    to = pl.ds(pl.multiple_of((1 - core) * half, half), half)
    stats = [in_ref[q, sub:, :].astype(F32) for q in range(n_rep)]
    off, scale = whole([three(s, 0) for s in stats], [three(s, 3) for s in stats], samples)
    pieces = sems.shape[0]
    step = sub // pieces
    copies = []
    for i in range(pieces):
        at = slice(i * step, (i + 1) * step)
        total = joined([in_ref[q, at, :] for q in range(n_rep)], off, scale, turned_ref[at, :], samples)
        held_ref[at, :] = total
        copies.append(pltpu.make_async_copy(held_ref.at[at, :], main_ref.at[at, to], sems.at[i]))
        copies[-1].start()
    for copy in copies:
        copy.wait()


def steps(genotypes):
    sample_rows, variants = genotypes.shape
    n_row, n_col, n_rep = (lax.axis_size(a) for a in ("row", "col", "rep"))
    width = variants // n_row
    half, slab = width // 2, width // n_col
    pairs = n_row * n_col
    samples = sample_rows * pairs
    sub = width // n_rep
    cols = half + slab
    shape = jax.ShapeDtypeStruct

    payload = pl.pallas_call(
        functools.partial(pack_body, n_row, n_col),
        out_shape=shape((pairs, sample_rows, half + cols), BF16),
        compiler_params=params(8),
        cost_estimate=cost(0, 4 * pairs * sample_rows * (half + cols)),
        name="pack",
    )(genotypes)
    arrived = lax.all_to_all(payload, ("row", "col"), 0, 0, tiled=True)

    to_pair, to_core, own = pl.pallas_call(
        split_body,
        out_shape=(
            shape((pairs, sample_rows, half), BF16),
            shape((pairs, sample_rows, half), BF16),
            shape((samples, half + cols), BF16),
        ),
        compiler_params=params(8),
        cost_estimate=cost(0, 8 * samples * (half + cols)),
        name="split",
    )(arrived)

    def mate(r, c):
        return ((r - 1) % n_row) * n_col + c + 1 if c % 2 == 0 else ((r + 1) % n_row) * n_col + c - 1

    mates = [(r * n_col + c, mate(r, c)) for r in range(n_row) for c in range(n_col)]
    swapped = lax.ppermute(to_pair, ("row", "col"), mates)
    other = lax.ppermute(to_core, "col", [(c, c ^ 1) for c in range(n_col)])
    left, across_fix, right_fix, foot, opposite = pl.pallas_call(
        tile_across,
        out_shape=(
            shape((samples, width), BF16),
            shape((8, sub), BF16),
            shape((8, cols), BF16),
            shape((8, cols), F32),
            shape((sub + 16, cols), BF16),
        ),
        compiler_params=params(16),
        cost_estimate=cost(2 * samples * sub * cols, 2 * samples * (2 * width + cols)),
        name="tile_across",
    )(own, other)
    opposite = lax.ppermute(opposite, "rep", [(q, (q + 2) % n_rep) for q in range(n_rep)])
    fix, *parts = pl.pallas_call(
        tile_others,
        out_shape=(shape((8, width), BF16), *[shape((sub + 16, cols), BF16)] * (n_rep - 1)),
        compiler_params=params(16),
        cost_estimate=cost(6 * samples * sub * cols, 2 * samples * (width + cols)),
        name="tile_others",
    )(left, across_fix, right_fix, foot, own)
    parts[1] = lax.ppermute(parts[1], "rep", [(q, q ^ 1) for q in range(n_rep)])
    parts[2] = lax.ppermute(parts[2], "rep", [(q, n_rep - 1 - q) for q in range(n_rep)])
    parts.append(opposite)
    partial = pl.pallas_call(
        tile_second,
        out_shape=shape((n_rep, sub + 8, half), BF16),
        out_specs=pl.BlockSpec(memory_space=pl.ANY),
        scratch_shapes=[pltpu.VMEM((n_rep, sub + 8, half), BF16), pltpu.SemaphoreType.DMA((n_rep,))],
        compiler_params=params(16),
        cost_estimate=cost(2 * samples * width * half, 2 * samples * (width + half)),
        name="tile_second",
    )(left, fix, swapped)
    got = lax.all_to_all(partial, "rep", 0, 0, tiled=True)
    vmem = pl.BlockSpec(memory_space=pltpu.VMEM)
    far_off = pl.BlockSpec(memory_space=pltpu.HBM)
    turned, main, far = pl.pallas_call(
        functools.partial(join_first, samples),
        out_shape=(shape((sub, 8), F32), shape((sub, width), F32), shape((sub, slab), F32)),
        out_specs=(vmem, far_off, vmem),
        scratch_shapes=[pltpu.VMEM((sub, half), F32), pltpu.SemaphoreType.DMA],
        compiler_params=params(8),
        cost_estimate=cost(12 * sub * cols, 12 * sub * cols),
        name="join_first",
    )(*parts)
    main = pl.pallas_call(
        functools.partial(join_second, samples),
        out_shape=shape((sub, width), F32),
        in_specs=[vmem, vmem, far_off],
        out_specs=far_off,
        scratch_shapes=[pltpu.VMEM((sub, half), F32), pltpu.SemaphoreType.DMA((4,))],
        input_output_aliases={2: 0},
        compiler_params=params(8),
        cost_estimate=cost(12 * sub * half, 12 * sub * half),
        name="join_second",
    )(got, turned, main)
    return main.reshape(1, 1, sub, width), far.reshape(1, sub, slab)


def solution(mesh):
    return jax.shard_map(
        steps,
        mesh=mesh,
        in_specs=(P(("row", "col", "rep"), None),),
        out_specs=(P("row", "col", "rep", None), P("row", "rep", "col")),
        check_vma=False,
    )
```

profile of v0, /device:TPU:1, one launch (start us, length us, event | category | flops | bytes accessed | tf_op | source)
XLA Modules:
  0.0 110.6 jit_solution(16264205117600230203)
XLA Ops:
  0.6 0.0 copy-start
  0.6 0.9 copy-done
  1.5 0.1 pack.1
  1.6 52.3 %all_to_all.10.in_ref = bf16[128,4,1152]{2,1,0:T(4,128)(2,1)S(1)} all-to-all(bf16[128,4,1152]{2,1,0:T(4,128)(2,1)S(1)} %pack.1), channel_id=1, replica_groups=mesh['row'=16,'col'=8,'rep'=4] {'row','col'}, dimensions={0} | all-to-all | bytes 2359296 | tf_op jit(solution)/shard_map/all_to_all | solution.py:221
  53.9 0.2 split.1
  54.1 1.9 %collective-permute-start = (bf16[128,4,512]{2,1,0:T(4,128)(2,1)S(1)}, bf16[128,4,512]{2,1,0:T(4,128)(2,1)S(1)}, u32[]{:S(2)}, u32[]{:S(2)}) collective-permute-start(bf16[128,4,512]{2,1,0:T(4,128)(2,1)S(1)} %get-tuple-element.18), channel_id=1, source_target_pairs={{0,4},{4,0},{8,12},{12,8},{16,20},{20,16},{24,28},{28,24},{1,5},{5... | collective-permute-start | bytes 1572872 | tf_op jit(solution)/shard_map/ppermute | solution.py:240
  56.1 2.8 %collective-permute-start.1 = (bf16[128,4,512]{2,1,0:T(4,128)(2,1)S(1)}, bf16[128,4,512]{2,1,0:T(4,128)(2,1)S(1)}, u32[]{:S(2)}, u32[]{:S(2)}) collective-permute-start(bf16[128,4,512]{2,1,0:T(4,128)(2,1)S(1)} %get-tuple-element.24), channel_id=1, source_target_pairs={{0,484},{4,32},{8,492},{12,40},{16,500},{20,48},{24,508},{28,56},{... | collective-permute-start | bytes 1572872 | tf_op jit(solution)/shard_map/ppermute | solution.py:239
  58.9 0.0 collective-permute-done.other_ref
  58.9 0.7 tile_across.1
  59.7 1.2 %tile_others.1 = (bf16[8,1024]{1,0:T(8,128)(2,1)S(1)}, bf16[272,640]{1,0:T(8,128)(2,1)S(1)}, bf16[272,640]{1,0:T(8,128)(2,1)S(1)}, bf16[272,640]{1,0:T(8,128)(2,1)S(1)}) custom-call(bf16[512,1024]{1,0:T(8,128)(2,1)S(1)} %get-tuple-element.19.left_ref, bf16[8,256]{1,0:T(8,128)(2,1)S(1)} %get-tuple-element.20.across_ref, ...), custom_call_target="tpu_custom_call" | custom-call | flops 503316480 | bytes 1703936 | tf_op jit(solution)/shard_map/tile_others/pallas_call | solution.py:255
  60.9 11.6 %collective-permute-done.1.swapped_ref = bf16[128,4,512]{2,1,0:T(4,128)(2,1)S(1)} collective-permute-done((bf16[128,4,512]{2,1,0:T(4,128)(2,1)S(1)}, bf16[128,4,512]{2,1,0:T(4,128)(2,1)S(1)}, u32[]{:S(2)}, u32[]{:S(2)}) %collective-permute-start.1) | collective-permute-done | bytes 524320 | tf_op jit(solution)/shard_map/ppermute | solution.py:239
  72.4 2.0 %tile_second.1 = bf16[4,264,512]{2,1,0:T(8,128)(2,1)} custom-call(bf16[512,1024]{1,0:T(8,128)(2,1)S(1)} %get-tuple-element.19.left_ref, bf16[8,1024]{1,0:T(8,128)(2,1)S(1)} %get-tuple-element.23.fix_ref, bf16[128,4,512]{2,1,0:T(4,128)(2,1)S(1)} %collective-permute-done.1.swapped_ref), custom_call_target="tpu_custom_call" | custom-call | flops 536870912 | bytes 1572864 | tf_op jit(solution)/shard_map/tile_second/pallas_call | solution.py:265
  74.4 4.0 %all-to-all-start.1 = ((bf16[4,264,512]{2,1,0:T(8,128)(2,1)}), bf16[4,264,512]{2,1,0:T(8,128)(2,1)S(1)}, u32[]{:S(2)}, u32[]{:S(2)}) async-start(bf16[4,264,512]{2,1,0:T(8,128)(2,1)} %tile_second.1), calls=%async_computation.1 | async-start | bytes 2162688 | tf_op jit(solution)/shard_map/all_to_all | solution.py:274
  78.5 3.4 %collective-permute-start.2 = (bf16[272,640]{1,0:T(8,128)(2,1)S(1)}, bf16[272,640]{1,0:T(8,128)(2,1)S(1)}, u32[]{:S(2)}, u32[]{:S(2)}) collective-permute-start(bf16[272,640]{1,0:T(8,128)(2,1)S(1)} %get-tuple-element.26), channel_id=1, source_target_pairs={{0,1},{1,0},{2,3},{3,2},{4,5},{5,4},{6,7},{7,6},{8,9},{9,8},{10,11... | collective-permute-start | bytes 1044488 | tf_op jit(solution)/shard_map/ppermute | solution.py:262
  81.8 3.7 %collective-permute-start.3 = (bf16[272,640]{1,0:T(8,128)(2,1)S(1)}, bf16[272,640]{1,0:T(8,128)(2,1)S(1)}, u32[]{:S(2)}, u32[]{:S(2)}) collective-permute-start(bf16[272,640]{1,0:T(8,128)(2,1)S(1)} %get-tuple-element.27), channel_id=1, source_target_pairs={{0,3},{1,2},{2,1},{3,0},{4,7},{5,6},{6,5},{7,4},{8,11},{9,10},{10,... | collective-permute-start | bytes 1044488 | tf_op jit(solution)/shard_map/ppermute | solution.py:263
  85.5 2.5 %collective-permute-start.4 = (bf16[272,640]{1,0:T(8,128)(2,1)S(1)}, bf16[272,640]{1,0:T(8,128)(2,1)S(1)}, u32[]{:S(2)}, u32[]{:S(2)}) collective-permute-start(bf16[272,640]{1,0:T(8,128)(2,1)S(1)} %get-tuple-element.28), channel_id=1, source_target_pairs={{0,2},{1,3},{2,0},{3,1},{4,6},{5,7},{6,4},{7,5},{8,10},{9,11},{10,... | collective-permute-start | bytes 1044488 | tf_op jit(solution)/shard_map/ppermute | solution.py:254
  88.1 10.4 %collective-permute-done.2.refs_1_ = bf16[272,640]{1,0:T(8,128)(2,1)S(1)} collective-permute-done((bf16[272,640]{1,0:T(8,128)(2,1)S(1)}, bf16[272,640]{1,0:T(8,128)(2,1)S(1)}, u32[]{:S(2)}, u32[]{:S(2)}) %collective-permute-start.2) | collective-permute-done | bytes 348192 | tf_op jit(solution)/shard_map/ppermute | solution.py:262
  98.5 2.4 %collective-permute-done.3.refs_2_ = bf16[272,640]{1,0:T(8,128)(2,1)S(1)} collective-permute-done((bf16[272,640]{1,0:T(8,128)(2,1)S(1)}, bf16[272,640]{1,0:T(8,128)(2,1)S(1)}, u32[]{:S(2)}, u32[]{:S(2)}) %collective-permute-start.3) | collective-permute-done | bytes 348192 | tf_op jit(solution)/shard_map/ppermute | solution.py:263
  100.9 6.6 %collective-permute-done.4.refs_3_ = bf16[272,640]{1,0:T(8,128)(2,1)S(1)} collective-permute-done((bf16[272,640]{1,0:T(8,128)(2,1)S(1)}, bf16[272,640]{1,0:T(8,128)(2,1)S(1)}, u32[]{:S(2)}, u32[]{:S(2)}) %collective-permute-start.4) | collective-permute-done | bytes 348192 | tf_op jit(solution)/shard_map/ppermute | solution.py:254
  107.4 2.0 %join_first.1 = (f32[256,8]{1,0:T(8,128)S(1)}, f32[256,1024]{1,0:T(8,128)}, f32[256,128]{1,0:T(8,128)}) custom-call(bf16[272,640]{1,0:T(8,128)(2,1)S(1)} %get-tuple-element.25.refs_0_, bf16[272,640]{1,0:T(8,128)(2,1)S(1)} %collective-permute-done.2.refs_1_, bf16[272,640]{1,0:T(8,128)(2,1)S(1)} %collective-permute-done.3.refs_2_, ...), custom_call_target="tpu_custom_call" | custom-call | flops 1966080 | bytes 1966080 | tf_op jit(solution)/shard_map/join_first/pallas_call | solution.py:277
  109.5 0.0 all-to-all-done.1.in_ref
  109.5 1.1 join_second.1
Async XLA Ops:
  0.6 0.9 copy-start
  54.1 4.7 %collective-permute-start = (bf16[128,4,512]{2,1,0:T(4,128)(2,1)S(1)}, bf16[128,4,512]{2,1,0:T(4,128)(2,1)S(1)}, u32[]{:S(2)}, u32[]{:S(2)}) collective-permute-start(bf16[128,4,512]{2,1,0:T(4,128)(2,1)S(1)} %get-tuple-element.18), channel_id=1, source_target_pairs={{0,4},{4,0},{8,12},{12,8},{16,20},{20,16},{24,28},{28,24},{1,5},{5... | collective-permute-start | bytes 1572872 | tf_op jit(solution)/shard_map/ppermute | solution.py:240
  56.1 16.3 %collective-permute-start.1 = (bf16[128,4,512]{2,1,0:T(4,128)(2,1)S(1)}, bf16[128,4,512]{2,1,0:T(4,128)(2,1)S(1)}, u32[]{:S(2)}, u32[]{:S(2)}) collective-permute-start(bf16[128,4,512]{2,1,0:T(4,128)(2,1)S(1)} %get-tuple-element.24), channel_id=1, source_target_pairs={{0,484},{4,32},{8,492},{12,40},{16,500},{20,48},{24,508},{28,56},{... | collective-permute-start | bytes 1572872 | tf_op jit(solution)/shard_map/ppermute | solution.py:239
  74.4 35.0 %all-to-all-start.1 = ((bf16[4,264,512]{2,1,0:T(8,128)(2,1)}), bf16[4,264,512]{2,1,0:T(8,128)(2,1)S(1)}, u32[]{:S(2)}, u32[]{:S(2)}) async-start(bf16[4,264,512]{2,1,0:T(8,128)(2,1)} %tile_second.1), calls=%async_computation.1 | async-start | bytes 2162688 | tf_op jit(solution)/shard_map/all_to_all | solution.py:274
  78.5 20.0 %collective-permute-start.2 = (bf16[272,640]{1,0:T(8,128)(2,1)S(1)}, bf16[272,640]{1,0:T(8,128)(2,1)S(1)}, u32[]{:S(2)}, u32[]{:S(2)}) collective-permute-start(bf16[272,640]{1,0:T(8,128)(2,1)S(1)} %get-tuple-element.26), channel_id=1, source_target_pairs={{0,1},{1,0},{2,3},{3,2},{4,5},{5,4},{6,7},{7,6},{8,9},{9,8},{10,11... | collective-permute-start | bytes 1044488 | tf_op jit(solution)/shard_map/ppermute | solution.py:262
  81.8 19.0 %collective-permute-start.3 = (bf16[272,640]{1,0:T(8,128)(2,1)S(1)}, bf16[272,640]{1,0:T(8,128)(2,1)S(1)}, u32[]{:S(2)}, u32[]{:S(2)}) collective-permute-start(bf16[272,640]{1,0:T(8,128)(2,1)S(1)} %get-tuple-element.27), channel_id=1, source_target_pairs={{0,3},{1,2},{2,1},{3,0},{4,7},{5,6},{6,5},{7,4},{8,11},{9,10},{10,... | collective-permute-start | bytes 1044488 | tf_op jit(solution)/shard_map/ppermute | solution.py:263
  85.5 21.9 %collective-permute-start.4 = (bf16[272,640]{1,0:T(8,128)(2,1)S(1)}, bf16[272,640]{1,0:T(8,128)(2,1)S(1)}, u32[]{:S(2)}, u32[]{:S(2)}) collective-permute-start(bf16[272,640]{1,0:T(8,128)(2,1)S(1)} %get-tuple-element.28), channel_id=1, source_target_pairs={{0,2},{1,3},{2,0},{3,1},{4,6},{5,7},{6,4},{7,5},{8,10},{9,11},{10,... | collective-permute-start | bytes 1044488 | tf_op jit(solution)/shard_map/ppermute | solution.py:254
where the time goes:
time: 111 us
  blocking collectives  52.3 us (47%)
  waiting for transfers between devices  30.9 us (28%)
  starting transfers between devices  18.3 us (16%)
  Pallas kernels  7.41 us (7%)
    all_to_all x1, blocking collectives, steps(): arrived = lax.all_to_all(payload, ('row', 'col'), 0, 0, tiled=True)  52.3 us
    ppermute x1, waiting for transfers between devices, steps(): swapped = lax.ppermute(to_pair, ('row', 'col'), mates)  11.6 us
    ppermute x1, waiting for transfers between devices, steps(): parts[1] = lax.ppermute(parts[1], 'rep', [(q, q ^ 1) for q in range(n_rep)])  10.4 us
    ppermute x1, waiting for transfers between devices, steps(): lax.ppermute(opposite, 'rep', [(q, (q + 2) % n_rep) for q in range(n_rep)])  6.59 us
    all_to_all x1, starting transfers between devices, steps(): got = lax.all_to_all(partial, 'rep', 0, 0, tiled=True)  4.02 us
    ppermute x1, starting transfers between devices, steps(): lax.ppermute(parts[2], 'rep', [(q, n_rep - 1 - q) for q in range(n_rep)])  3.7 us
    ppermute x1, starting transfers between devices, steps(): parts[1] = lax.ppermute(parts[1], 'rep', [(q, q ^ 1) for q in range(n_rep)])  3.36 us
    ppermute x1, starting transfers between devices, steps(): swapped = lax.ppermute(to_pair, ('row', 'col'), mates)  2.81 us
  transfers between devices with their start and end apart: 6, of which 4 were waited for; matrix products, arithmetic and copies ran while one was open for 0% of the time, Pallas kernels for 4%

commit v1 on v0

--- a/solution.py
+++ b/solution.py
@@ -107,13 +107,21 @@
     fix_ref[...] = piece(q, left_ref, right, right_fix, foot, out_ref)
 
 
-def tile_others(left_ref, across_ref, right_fix_ref, foot_ref, own_ref, fix_ref, *out_refs):
-    sub, half = across_ref.shape[1], left_ref.shape[1] // 2
-    *near, opposite = partners(lax.axis_index("rep"))
-    fix_ref[:, pl.ds(pl.multiple_of(opposite * sub, sub), sub)] = across_ref[...]
+def tile_near(left_ref, right_fix_ref, foot_ref, own_ref, fix_a_ref, fix_b_ref, a_ref, b_ref):
+    half = left_ref.shape[1] // 2
+    _, near_a, near_b, _ = partners(lax.axis_index("rep"))
     right, right_fix, foot = own_ref[:, half:], right_fix_ref[...], foot_ref[...]
-    for q, ref in zip((near[1], near[2], near[0]), (out_refs[1], out_refs[2], out_refs[0])):
-        fix_ref[:, pl.ds(pl.multiple_of(q * sub, sub), sub)] = piece(q, left_ref, right, right_fix, foot, ref)
+    fix_a_ref[...] = piece(near_a, left_ref, right, right_fix, foot, a_ref)
+    fix_b_ref[...] = piece(near_b, left_ref, right, right_fix, foot, b_ref)
+
+
+def tile_self(left_ref, right_fix_ref, foot_ref, own_ref, a_ref, b_ref, c_ref, fix_ref, out_ref):
+    sub, half = a_ref.shape[1], left_ref.shape[1] // 2
+    mine, *others = partners(lax.axis_index("rep"))
+    right, right_fix, foot = own_ref[:, half:], right_fix_ref[...], foot_ref[...]
+    fixes = [piece(mine, left_ref, right, right_fix, foot, out_ref), a_ref[...], b_ref[...], c_ref[...]]
+    for q, fix in zip((mine, *others), fixes):
+        fix_ref[:, pl.ds(pl.multiple_of(q * sub, sub), sub)] = fix
 
 
 def tile_second(left_ref, fix_ref, swapped_ref, out_ref, held_ref, sems):
@@ -252,16 +260,23 @@
         name="tile_across",
     )(own, other)
     opposite = lax.ppermute(opposite, "rep", [(q, (q + 2) % n_rep) for q in range(n_rep)])
-    fix, *parts = pl.pallas_call(
-        tile_others,
-        out_shape=(shape((8, width), BF16), *[shape((sub + 16, cols), BF16)] * (n_rep - 1)),
+    fix_a, fix_b, near_a, near_b = pl.pallas_call(
+        tile_near,
+        out_shape=(*[shape((8, sub), BF16)] * 2, *[shape((sub + 16, cols), BF16)] * 2),
         compiler_params=params(16),
-        cost_estimate=cost(6 * samples * sub * cols, 2 * samples * (width + cols)),
-        name="tile_others",
-    )(left, across_fix, right_fix, foot, own)
-    parts[1] = lax.ppermute(parts[1], "rep", [(q, q ^ 1) for q in range(n_rep)])
-    parts[2] = lax.ppermute(parts[2], "rep", [(q, n_rep - 1 - q) for q in range(n_rep)])
-    parts.append(opposite)
+        cost_estimate=cost(4 * samples * sub * cols, 2 * samples * (width + cols)),
+        name="tile_near",
+    )(left, right_fix, foot, own)
+    near_a = lax.ppermute(near_a, "rep", [(q, q ^ 1) for q in range(n_rep)])
+    near_b = lax.ppermute(near_b, "rep", [(q, n_rep - 1 - q) for q in range(n_rep)])
+    fix, mine = pl.pallas_call(
+        tile_self,
+        out_shape=(shape((8, width), BF16), shape((sub + 16, cols), BF16)),
+        compiler_params=params(16),
+        cost_estimate=cost(2 * samples * sub * cols, 2 * samples * (width + cols)),
+        name="tile_self",
+    )(left, right_fix, foot, own, fix_a, fix_b, across_fix)
+    parts = [mine, near_a, near_b, opposite]
     partial = pl.pallas_call(
         tile_second,
         out_shape=shape((n_rep, sub + 8, half), BF16),

time: 111 us -> 113 us (1.018)
  waiting for transfers between devices: 30.9 us -> 32.5 us
    ppermute x1, waiting for transfers between devices: 6.59 us -> 11.9 us  [steps(): lax.ppermute(opposite, 'rep', [(q, (q + 2) % n_rep) for q in range(n_rep)])]
    ppermute x2, waiting for transfers between devices: 12.8 us -> 9.33 us  [the longest x1 5.96 us: steps(): near_a = lax.ppermute(near_a, 'rep', [(q, q ^ 1) for q in range(n_rep)])]
    ppermute x2, starting transfers between devices: 7.06 us -> 4.72 us  [the longest x1 2.52 us: steps(): lax.ppermute(near_b, 'rep', [(q, n_rep - 1 - q) for q in range(n_rep)])]
    ppermute x1, starting transfers between devices: 2.53 us -> 4.86 us  [steps(): lax.ppermute(opposite, 'rep', [(q, (q + 2) % n_rep) for q in range(n_rep)])]
where the time goes in v1:
time: 113 us; the launch traced here: 112 us
  blocking collectives  52.3 us (46%)
  waiting for transfers between devices  32.5 us (29%)
  starting transfers between devices  18.3 us (16%)
  Pallas kernels  7.72 us (7%)
    all_to_all x1, blocking collectives, steps(): arrived = lax.all_to_all(payload, ('row', 'col'), 0, 0, tiled=True)  52.3 us
    ppermute x1, waiting for transfers between devices, steps(): lax.ppermute(opposite, 'rep', [(q, (q + 2) % n_rep) for q in range(n_rep)])  11.9 us
    ppermute x1, waiting for transfers between devices, steps(): swapped = lax.ppermute(to_pair, ('row', 'col'), mates)  11.3 us
    ppermute x1, waiting for transfers between devices, steps(): near_a = lax.ppermute(near_a, 'rep', [(q, q ^ 1) for q in range(n_rep)])  5.96 us
    ppermute x1, starting transfers between devices, steps(): lax.ppermute(opposite, 'rep', [(q, (q + 2) % n_rep) for q in range(n_rep)])  4.86 us
    all_to_all x1, starting transfers between devices, steps(): got = lax.all_to_all(partial, 'rep', 0, 0, tiled=True)  4.02 us
    ppermute x1, waiting for transfers between devices, steps(): lax.ppermute(near_b, 'rep', [(q, n_rep - 1 - q) for q in range(n_rep)])  3.37 us
    ppermute x1, starting transfers between devices, steps(): swapped = lax.ppermute(to_pair, ('row', 'col'), mates)  2.81 us
  transfers between devices with their start and end apart: 6, of which 4 were waited for; matrix products, arithmetic and copies ran while one was open for 0% of the time, Pallas kernels for 4%

profile of v1, /device:TPU:1, one launch (start us, length us, event | category | flops | bytes accessed | tf_op | source)
XLA Modules:
  0.0 112.5 jit_solution(10092907720163156050)
XLA Ops:
  0.6 0.0 copy-start
  0.6 0.9 copy-done
  1.5 0.1 pack.1
  1.6 52.3 %all_to_all.10.in_ref = bf16[128,4,1152]{2,1,0:T(4,128)(2,1)S(1)} all-to-all(bf16[128,4,1152]{2,1,0:T(4,128)(2,1)S(1)} %pack.1), channel_id=1, replica_groups=mesh['row'=16,'col'=8,'rep'=4] {'row','col'}, dimensions={0} | all-to-all | bytes 2359296 | tf_op jit(solution)/shard_map/all_to_all | solution.py:229
  53.9 0.2 split.1
  54.1 1.9 %collective-permute-start = (bf16[128,4,512]{2,1,0:T(4,128)(2,1)S(1)}, bf16[128,4,512]{2,1,0:T(4,128)(2,1)S(1)}, u32[]{:S(2)}, u32[]{:S(2)}) collective-permute-start(bf16[128,4,512]{2,1,0:T(4,128)(2,1)S(1)} %get-tuple-element.20), channel_id=1, source_target_pairs={{0,4},{4,0},{8,12},{12,8},{16,20},{20,16},{24,28},{28,24},{1,5},{5... | collective-permute-start | bytes 1572872 | tf_op jit(solution)/shard_map/ppermute | solution.py:248
  56.1 2.8 %collective-permute-start.1 = (bf16[128,4,512]{2,1,0:T(4,128)(2,1)S(1)}, bf16[128,4,512]{2,1,0:T(4,128)(2,1)S(1)}, u32[]{:S(2)}, u32[]{:S(2)}) collective-permute-start(bf16[128,4,512]{2,1,0:T(4,128)(2,1)S(1)} %get-tuple-element.28), channel_id=1, source_target_pairs={{0,484},{4,32},{8,492},{12,40},{16,500},{20,48},{24,508},{28,56},{... | collective-permute-start | bytes 1572872 | tf_op jit(solution)/shard_map/ppermute | solution.py:247
  58.9 0.0 collective-permute-done.other_ref
  58.9 0.8 tile_across.1
  59.7 0.9 tile_near.1
  60.5 0.6 tile_self.1
  61.2 11.3 %collective-permute-done.1.swapped_ref = bf16[128,4,512]{2,1,0:T(4,128)(2,1)S(1)} collective-permute-done((bf16[128,4,512]{2,1,0:T(4,128)(2,1)S(1)}, bf16[128,4,512]{2,1,0:T(4,128)(2,1)S(1)}, u32[]{:S(2)}, u32[]{:S(2)}) %collective-permute-start.1) | collective-permute-done | bytes 524320 | tf_op jit(solution)/shard_map/ppermute | solution.py:247
  72.4 2.1 %tile_second.1 = bf16[4,264,512]{2,1,0:T(8,128)(2,1)} custom-call(bf16[512,1024]{1,0:T(8,128)(2,1)S(1)} %get-tuple-element.21.left_ref, bf16[8,1024]{1,0:T(8,128)(2,1)S(1)} %get-tuple-element.27.fix_ref, bf16[128,4,512]{2,1,0:T(4,128)(2,1)S(1)} %collective-permute-done.1.swapped_ref), custom_call_target="tpu_custom_call" | custom-call | flops 536870912 | bytes 1572864 | tf_op jit(solution)/shard_map/tile_second/pallas_call | solution.py:280
  74.5 4.0 %all-to-all-start.1 = ((bf16[4,264,512]{2,1,0:T(8,128)(2,1)}), bf16[4,264,512]{2,1,0:T(8,128)(2,1)S(1)}, u32[]{:S(2)}, u32[]{:S(2)}) async-start(bf16[4,264,512]{2,1,0:T(8,128)(2,1)} %tile_second.1), calls=%async_computation.1 | async-start | bytes 2162688 | tf_op jit(solution)/shard_map/all_to_all | solution.py:289
  78.5 4.9 %collective-permute-start.4 = (bf16[272,640]{1,0:T(8,128)(2,1)S(1)}, bf16[272,640]{1,0:T(8,128)(2,1)S(1)}, u32[]{:S(2)}, u32[]{:S(2)}) collective-permute-start(bf16[272,640]{1,0:T(8,128)(2,1)S(1)} %get-tuple-element.32), channel_id=1, source_target_pairs={{0,2},{1,3},{2,0},{3,1},{4,6},{5,7},{6,4},{7,5},{8,10},{9,11},{10,... | collective-permute-start | bytes 1044488 | tf_op jit(solution)/shard_map/ppermute | solution.py:262
  83.4 2.2 %collective-permute-start.2 = (bf16[272,640]{1,0:T(8,128)(2,1)S(1)}, bf16[272,640]{1,0:T(8,128)(2,1)S(1)}, u32[]{:S(2)}, u32[]{:S(2)}) collective-permute-start(bf16[272,640]{1,0:T(8,128)(2,1)S(1)} %get-tuple-element.30), channel_id=1, source_target_pairs={{0,1},{1,0},{2,3},{3,2},{4,5},{5,4},{6,7},{7,6},{8,9},{9,8},{10,11... | collective-permute-start | bytes 1044488 | tf_op jit(solution)/shard_map/ppermute | solution.py:270
  85.6 2.5 %collective-permute-start.3 = (bf16[272,640]{1,0:T(8,128)(2,1)S(1)}, bf16[272,640]{1,0:T(8,128)(2,1)S(1)}, u32[]{:S(2)}, u32[]{:S(2)}) collective-permute-start(bf16[272,640]{1,0:T(8,128)(2,1)S(1)} %get-tuple-element.31), channel_id=1, source_target_pairs={{0,3},{1,2},{2,1},{3,0},{4,7},{5,6},{6,5},{7,4},{8,11},{9,10},{10,... | collective-permute-start | bytes 1044488 | tf_op jit(solution)/shard_map/ppermute | solution.py:271
  88.1 11.9 %collective-permute-done.4.refs_3_ = bf16[272,640]{1,0:T(8,128)(2,1)S(1)} collective-permute-done((bf16[272,640]{1,0:T(8,128)(2,1)S(1)}, bf16[272,640]{1,0:T(8,128)(2,1)S(1)}, u32[]{:S(2)}, u32[]{:S(2)}) %collective-permute-start.4) | collective-permute-done | bytes 348192 | tf_op jit(solution)/shard_map/ppermute | solution.py:262
  100.0 6.0 %collective-permute-done.2.refs_1_ = bf16[272,640]{1,0:T(8,128)(2,1)S(1)} collective-permute-done((bf16[272,640]{1,0:T(8,128)(2,1)S(1)}, bf16[272,640]{1,0:T(8,128)(2,1)S(1)}, u32[]{:S(2)}, u32[]{:S(2)}) %collective-permute-start.2) | collective-permute-done | bytes 348192 | tf_op jit(solution)/shard_map/ppermute | solution.py:270
  106.0 3.4 %collective-permute-done.3.refs_2_ = bf16[272,640]{1,0:T(8,128)(2,1)S(1)} collective-permute-done((bf16[272,640]{1,0:T(8,128)(2,1)S(1)}, bf16[272,640]{1,0:T(8,128)(2,1)S(1)}, u32[]{:S(2)}, u32[]{:S(2)}) %collective-permute-start.3) | collective-permute-done | bytes 348192 | tf_op jit(solution)/shard_map/ppermute | solution.py:271
  109.3 2.0 %join_first.1 = (f32[256,8]{1,0:T(8,128)S(1)}, f32[256,1024]{1,0:T(8,128)}, f32[256,128]{1,0:T(8,128)}) custom-call(bf16[272,640]{1,0:T(8,128)(2,1)S(1)} %get-tuple-element.29.refs_0_, bf16[272,640]{1,0:T(8,128)(2,1)S(1)} %collective-permute-done.2.refs_1_, bf16[272,640]{1,0:T(8,128)(2,1)S(1)} %collective-permute-done.3.refs_2_, ...), custom_call_target="tpu_custom_call" | custom-call | flops 1966080 | bytes 1966080 | tf_op jit(solution)/shard_map/join_first/pallas_call | solution.py:292
  111.4 0.0 all-to-all-done.1.in_ref
  111.4 1.1 join_second.1
Async XLA Ops:
  0.6 0.9 copy-start
  54.1 4.7 %collective-permute-start = (bf16[128,4,512]{2,1,0:T(4,128)(2,1)S(1)}, bf16[128,4,512]{2,1,0:T(4,128)(2,1)S(1)}, u32[]{:S(2)}, u32[]{:S(2)}) collective-permute-start(bf16[128,4,512]{2,1,0:T(4,128)(2,1)S(1)} %get-tuple-element.20), channel_id=1, source_target_pairs={{0,4},{4,0},{8,12},{12,8},{16,20},{20,16},{24,28},{28,24},{1,5},{5... | collective-permute-start | bytes 1572872 | tf_op jit(solution)/shard_map/ppermute | solution.py:248
  56.1 16.3 %collective-permute-start.1 = (bf16[128,4,512]{2,1,0:T(4,128)(2,1)S(1)}, bf16[128,4,512]{2,1,0:T(4,128)(2,1)S(1)}, u32[]{:S(2)}, u32[]{:S(2)}) collective-permute-start(bf16[128,4,512]{2,1,0:T(4,128)(2,1)S(1)} %get-tuple-element.28), channel_id=1, source_target_pairs={{0,484},{4,32},{8,492},{12,40},{16,500},{20,48},{24,508},{28,56},{... | collective-permute-start | bytes 1572872 | tf_op jit(solution)/shard_map/ppermute | solution.py:247
  74.5 36.9 %all-to-all-start.1 = ((bf16[4,264,512]{2,1,0:T(8,128)(2,1)}), bf16[4,264,512]{2,1,0:T(8,128)(2,1)S(1)}, u32[]{:S(2)}, u32[]{:S(2)}) async-start(bf16[4,264,512]{2,1,0:T(8,128)(2,1)} %tile_second.1), calls=%async_computation.1 | async-start | bytes 2162688 | tf_op jit(solution)/shard_map/all_to_all | solution.py:289
  78.5 21.5 %collective-permute-start.4 = (bf16[272,640]{1,0:T(8,128)(2,1)S(1)}, bf16[272,640]{1,0:T(8,128)(2,1)S(1)}, u32[]{:S(2)}, u32[]{:S(2)}) collective-permute-start(bf16[272,640]{1,0:T(8,128)(2,1)S(1)} %get-tuple-element.32), channel_id=1, source_target_pairs={{0,2},{1,3},{2,0},{3,1},{4,6},{5,7},{6,4},{7,5},{8,10},{9,11},{10,... | collective-permute-start | bytes 1044488 | tf_op jit(solution)/shard_map/ppermute | solution.py:262
  83.4 22.6 %collective-permute-start.2 = (bf16[272,640]{1,0:T(8,128)(2,1)S(1)}, bf16[272,640]{1,0:T(8,128)(2,1)S(1)}, u32[]{:S(2)}, u32[]{:S(2)}) collective-permute-start(bf16[272,640]{1,0:T(8,128)(2,1)S(1)} %get-tuple-element.30), channel_id=1, source_target_pairs={{0,1},{1,0},{2,3},{3,2},{4,5},{5,4},{6,7},{7,6},{8,9},{9,8},{10,11... | collective-permute-start | bytes 1044488 | tf_op jit(solution)/shard_map/ppermute | solution.py:270
  85.6 23.8 %collective-permute-start.3 = (bf16[272,640]{1,0:T(8,128)(2,1)S(1)}, bf16[272,640]{1,0:T(8,128)(2,1)S(1)}, u32[]{:S(2)}, u32[]{:S(2)}) collective-permute-start(bf16[272,640]{1,0:T(8,128)(2,1)S(1)} %get-tuple-element.31), channel_id=1, source_target_pairs={{0,3},{1,2},{2,1},{3,0},{4,7},{5,6},{6,5},{7,4},{8,11},{9,10},{10,... | collective-permute-start | bytes 1044488 | tf_op jit(solution)/shard_map/ppermute | solution.py:271

commit v2 on v1

--- a/solution.py
+++ b/solution.py
@@ -78,18 +78,22 @@
 
 def piece(q, left_ref, right, right_fix, foot, out_ref):
     rows, cols = out_ref.shape
-    sub, samples = rows - 16, left_ref.shape[0]
+    sub, samples = rows - 8, left_ref.shape[0]
     left = left_ref[:, pl.ds(pl.multiple_of(q * sub, sub), sub)]
     dose, square = sums(left)
     hi, mid, lo = thirds(dose)
     left_fix = stacked([hi, hi, mid, mid, hi, lo], 8).astype(BF16)
     mean = dose / samples
-    gap = jnp.zeros((1, cols - sub), F32)
-    mine = [*thirds(mean), *thirds(square - dose * mean)]
-    mine = [jnp.concatenate([v, gap], axis=1) for v in mine]
+    hi, mid, lo = thirds(mean)
+    top, low, _ = thirds(square - dose * mean)
+    rest = cols - 2 * sub
+    mine = [
+        jnp.concatenate([hi, mid, lo[:, :rest]], axis=1),
+        jnp.concatenate([top, low, lo[:, sub - rest :]], axis=1),
+    ]
     part = dot0(left, right) + dot0(left_fix, right_fix)
     out_ref[:sub, :] = part.astype(BF16)
-    out_ref[sub:, :] = stacked([foot[:6], *mine], 16, 12).astype(BF16)
+    out_ref[sub:, :] = jnp.concatenate([foot[:6], *mine], axis=0).astype(BF16)
     return left_fix
 
 
@@ -167,9 +171,10 @@
     sub, near = near_ref.shape
     n_rep = len(in_refs)
     stats = [r[sub:, :].astype(F32) for r in in_refs]
-    l_off, l_scale = whole(
-        [three(s[:, :sub], 6) for s in stats], [three(s[:, :sub], 9) for s in stats], samples
-    )
+    last = [jnp.concatenate([s[6:7, 2 * sub :], s[7:8, 2 * sub :]], axis=1) for s in stats]
+    pair = lambda s, i: s[i : i + 1, :sub] + s[i : i + 1, sub : 2 * sub]
+    l_mean = [pair(s, 6) + v for s, v in zip(stats, last)]
+    l_off, l_scale = whole(l_mean, [pair(s, 7) for s in stats], samples)
     l_scale = l_scale / (n_rep * samples)
     turned = stacked(l_off + [l_scale], 8).T
     off, scale = whole([three(s, 0) for s in stats], [three(s, 3) for s in stats], samples)
@@ -253,7 +258,7 @@
             shape((8, sub), BF16),
             shape((8, cols), BF16),
             shape((8, cols), F32),
-            shape((sub + 16, cols), BF16),
+            shape((sub + 8, cols), BF16),
         ),
         compiler_params=params(16),
         cost_estimate=cost(2 * samples * sub * cols, 2 * samples * (2 * width + cols)),
@@ -262,7 +267,7 @@
     opposite = lax.ppermute(opposite, "rep", [(q, (q + 2) % n_rep) for q in range(n_rep)])
     fix_a, fix_b, near_a, near_b = pl.pallas_call(
         tile_near,
-        out_shape=(*[shape((8, sub), BF16)] * 2, *[shape((sub + 16, cols), BF16)] * 2),
+        out_shape=(*[shape((8, sub), BF16)] * 2, *[shape((sub + 8, cols), BF16)] * 2),
         compiler_params=params(16),
         cost_estimate=cost(4 * samples * sub * cols, 2 * samples * (width + cols)),
         name="tile_near",
@@ -271,7 +276,7 @@
     near_b = lax.ppermute(near_b, "rep", [(q, n_rep - 1 - q) for q in range(n_rep)])
     fix, mine = pl.pallas_call(
         tile_self,
-        out_shape=(shape((8, width), BF16), shape((sub + 16, cols), BF16)),
+        out_shape=(shape((8, width), BF16), shape((sub + 8, cols), BF16)),
         compiler_params=params(16),
         cost_estimate=cost(2 * samples * sub * cols, 2 * samples * (width + cols)),
         name="tile_self",

time: 113 us -> 112 us (level)
  no operation moved by 1% of the time
where the time goes in v2:
time: 112 us
  blocking collectives  52.3 us (47%)
  waiting for transfers between devices  32.1 us (29%)
  starting transfers between devices  18.3 us (16%)
  Pallas kernels  7.68 us (7%)
    all_to_all x1, blocking collectives, steps(): arrived = lax.all_to_all(payload, ('row', 'col'), 0, 0, tiled=True)  52.3 us
    ppermute x1, waiting for transfers between devices, steps(): lax.ppermute(opposite, 'rep', [(q, (q + 2) % n_rep) for q in range(n_rep)])  11.7 us
    ppermute x1, waiting for transfers between devices, steps(): swapped = lax.ppermute(to_pair, ('row', 'col'), mates)  11.3 us
    ppermute x1, waiting for transfers between devices, steps(): near_a = lax.ppermute(near_a, 'rep', [(q, q ^ 1) for q in range(n_rep)])  5.74 us
    ppermute x1, starting transfers between devices, steps(): lax.ppermute(opposite, 'rep', [(q, (q + 2) % n_rep) for q in range(n_rep)])  4.86 us
    all_to_all x1, starting transfers between devices, steps(): got = lax.all_to_all(partial, 'rep', 0, 0, tiled=True)  4.02 us
    ppermute x1, waiting for transfers between devices, steps(): lax.ppermute(near_b, 'rep', [(q, n_rep - 1 - q) for q in range(n_rep)])  3.37 us
    ppermute x1, starting transfers between devices, steps(): swapped = lax.ppermute(to_pair, ('row', 'col'), mates)  2.81 us
  transfers between devices with their start and end apart: 6, of which 4 were waited for; matrix products, arithmetic and copies ran while one was open for 0% of the time, Pallas kernels for 4%

profile of v2, /device:TPU:1, one launch (start us, length us, event | category | flops | bytes accessed | tf_op | source)
XLA Modules:
  0.0 112.0 jit_solution(16753175347432510753)
XLA Ops:
  0.6 0.0 copy-start
  0.6 0.9 copy-done
  1.5 0.1 pack.1
  1.6 52.3 %all_to_all.10.in_ref = bf16[128,4,1152]{2,1,0:T(4,128)(2,1)S(1)} all-to-all(bf16[128,4,1152]{2,1,0:T(4,128)(2,1)S(1)} %pack.1), channel_id=1, replica_groups=mesh['row'=16,'col'=8,'rep'=4] {'row','col'}, dimensions={0} | all-to-all | bytes 2359296 | tf_op jit(solution)/shard_map/all_to_all | solution.py:234
  53.9 0.2 split.1
  54.1 1.9 %collective-permute-start = (bf16[128,4,512]{2,1,0:T(4,128)(2,1)S(1)}, bf16[128,4,512]{2,1,0:T(4,128)(2,1)S(1)}, u32[]{:S(2)}, u32[]{:S(2)}) collective-permute-start(bf16[128,4,512]{2,1,0:T(4,128)(2,1)S(1)} %get-tuple-element.20), channel_id=1, source_target_pairs={{0,4},{4,0},{8,12},{12,8},{16,20},{20,16},{24,28},{28,24},{1,5},{5... | collective-permute-start | bytes 1572872 | tf_op jit(solution)/shard_map/ppermute | solution.py:253
  56.1 2.8 %collective-permute-start.1 = (bf16[128,4,512]{2,1,0:T(4,128)(2,1)S(1)}, bf16[128,4,512]{2,1,0:T(4,128)(2,1)S(1)}, u32[]{:S(2)}, u32[]{:S(2)}) collective-permute-start(bf16[128,4,512]{2,1,0:T(4,128)(2,1)S(1)} %get-tuple-element.28), channel_id=1, source_target_pairs={{0,484},{4,32},{8,492},{12,40},{16,500},{20,48},{24,508},{28,56},{... | collective-permute-start | bytes 1572872 | tf_op jit(solution)/shard_map/ppermute | solution.py:252
  58.9 0.0 collective-permute-done.other_ref
  58.9 0.7 tile_across.1
  59.6 0.9 tile_near.1
  60.5 0.6 tile_self.1
  61.1 11.3 %collective-permute-done.1.swapped_ref = bf16[128,4,512]{2,1,0:T(4,128)(2,1)S(1)} collective-permute-done((bf16[128,4,512]{2,1,0:T(4,128)(2,1)S(1)}, bf16[128,4,512]{2,1,0:T(4,128)(2,1)S(1)}, u32[]{:S(2)}, u32[]{:S(2)}) %collective-permute-start.1) | collective-permute-done | bytes 524320 | tf_op jit(solution)/shard_map/ppermute | solution.py:252
  72.4 2.0 %tile_second.1 = bf16[4,264,512]{2,1,0:T(8,128)(2,1)} custom-call(bf16[512,1024]{1,0:T(8,128)(2,1)S(1)} %get-tuple-element.21.left_ref, bf16[8,1024]{1,0:T(8,128)(2,1)S(1)} %get-tuple-element.27.fix_ref, bf16[128,4,512]{2,1,0:T(4,128)(2,1)S(1)} %collective-permute-done.1.swapped_ref), custom_call_target="tpu_custom_call" | custom-call | flops 536870912 | bytes 1572864 | tf_op jit(solution)/shard_map/tile_second/pallas_call | solution.py:285
  74.5 4.0 %all-to-all-start.1 = ((bf16[4,264,512]{2,1,0:T(8,128)(2,1)}), bf16[4,264,512]{2,1,0:T(8,128)(2,1)S(1)}, u32[]{:S(2)}, u32[]{:S(2)}) async-start(bf16[4,264,512]{2,1,0:T(8,128)(2,1)} %tile_second.1), calls=%async_computation.1 | async-start | bytes 2162688 | tf_op jit(solution)/shard_map/all_to_all | solution.py:294
  78.5 4.9 %collective-permute-start.4 = (bf16[264,640]{1,0:T(8,128)(2,1)S(1)}, bf16[264,640]{1,0:T(8,128)(2,1)S(1)}, u32[]{:S(2)}, u32[]{:S(2)}) collective-permute-start(bf16[264,640]{1,0:T(8,128)(2,1)S(1)} %get-tuple-element.32), channel_id=1, source_target_pairs={{0,2},{1,3},{2,0},{3,1},{4,6},{5,7},{6,4},{7,5},{8,10},{9,11},{10,... | collective-permute-start | bytes 1013768 | tf_op jit(solution)/shard_map/ppermute | solution.py:267
  83.4 2.2 %collective-permute-start.2 = (bf16[264,640]{1,0:T(8,128)(2,1)S(1)}, bf16[264,640]{1,0:T(8,128)(2,1)S(1)}, u32[]{:S(2)}, u32[]{:S(2)}) collective-permute-start(bf16[264,640]{1,0:T(8,128)(2,1)S(1)} %get-tuple-element.30), channel_id=1, source_target_pairs={{0,1},{1,0},{2,3},{3,2},{4,5},{5,4},{6,7},{7,6},{8,9},{9,8},{10,11... | collective-permute-start | bytes 1013768 | tf_op jit(solution)/shard_map/ppermute | solution.py:275
  85.6 2.5 %collective-permute-start.3 = (bf16[264,640]{1,0:T(8,128)(2,1)S(1)}, bf16[264,640]{1,0:T(8,128)(2,1)S(1)}, u32[]{:S(2)}, u32[]{:S(2)}) collective-permute-start(bf16[264,640]{1,0:T(8,128)(2,1)S(1)} %get-tuple-element.31), channel_id=1, source_target_pairs={{0,3},{1,2},{2,1},{3,0},{4,7},{5,6},{6,5},{7,4},{8,11},{9,10},{10,... | collective-permute-start | bytes 1013768 | tf_op jit(solution)/shard_map/ppermute | solution.py:276
  88.1 11.7 %collective-permute-done.4.refs_3_ = bf16[264,640]{1,0:T(8,128)(2,1)S(1)} collective-permute-done((bf16[264,640]{1,0:T(8,128)(2,1)S(1)}, bf16[264,640]{1,0:T(8,128)(2,1)S(1)}, u32[]{:S(2)}, u32[]{:S(2)}) %collective-permute-start.4) | collective-permute-done | bytes 337952 | tf_op jit(solution)/shard_map/ppermute | solution.py:267
  99.8 5.7 %collective-permute-done.2.refs_1_ = bf16[264,640]{1,0:T(8,128)(2,1)S(1)} collective-permute-done((bf16[264,640]{1,0:T(8,128)(2,1)S(1)}, bf16[264,640]{1,0:T(8,128)(2,1)S(1)}, u32[]{:S(2)}, u32[]{:S(2)}) %collective-permute-start.2) | collective-permute-done | bytes 337952 | tf_op jit(solution)/shard_map/ppermute | solution.py:275
  105.5 3.4 %collective-permute-done.3.refs_2_ = bf16[264,640]{1,0:T(8,128)(2,1)S(1)} collective-permute-done((bf16[264,640]{1,0:T(8,128)(2,1)S(1)}, bf16[264,640]{1,0:T(8,128)(2,1)S(1)}, u32[]{:S(2)}, u32[]{:S(2)}) %collective-permute-start.3) | collective-permute-done | bytes 337952 | tf_op jit(solution)/shard_map/ppermute | solution.py:276
  108.9 2.0 %join_first.1 = (f32[256,8]{1,0:T(8,128)S(1)}, f32[256,1024]{1,0:T(8,128)}, f32[256,128]{1,0:T(8,128)}) custom-call(bf16[264,640]{1,0:T(8,128)(2,1)S(1)} %get-tuple-element.29.refs_0_, bf16[264,640]{1,0:T(8,128)(2,1)S(1)} %collective-permute-done.2.refs_1_, bf16[264,640]{1,0:T(8,128)(2,1)S(1)} %collective-permute-done.3.refs_2_, ...), custom_call_target="tpu_custom_call" | custom-call | flops 1966080 | bytes 1966080 | tf_op jit(solution)/shard_map/join_first/pallas_call | solution.py:297
  110.9 0.0 all-to-all-done.1.in_ref
  110.9 1.1 join_second.1
Async XLA Ops:
  0.6 0.9 copy-start
  54.1 4.7 %collective-permute-start = (bf16[128,4,512]{2,1,0:T(4,128)(2,1)S(1)}, bf16[128,4,512]{2,1,0:T(4,128)(2,1)S(1)}, u32[]{:S(2)}, u32[]{:S(2)}) collective-permute-start(bf16[128,4,512]{2,1,0:T(4,128)(2,1)S(1)} %get-tuple-element.20), channel_id=1, source_target_pairs={{0,4},{4,0},{8,12},{12,8},{16,20},{20,16},{24,28},{28,24},{1,5},{5... | collective-permute-start | bytes 1572872 | tf_op jit(solution)/shard_map/ppermute | solution.py:253
  56.1 16.3 %collective-permute-start.1 = (bf16[128,4,512]{2,1,0:T(4,128)(2,1)S(1)}, bf16[128,4,512]{2,1,0:T(4,128)(2,1)S(1)}, u32[]{:S(2)}, u32[]{:S(2)}) collective-permute-start(bf16[128,4,512]{2,1,0:T(4,128)(2,1)S(1)} %get-tuple-element.28), channel_id=1, source_target_pairs={{0,484},{4,32},{8,492},{12,40},{16,500},{20,48},{24,508},{28,56},{... | collective-permute-start | bytes 1572872 | tf_op jit(solution)/shard_map/ppermute | solution.py:252
  74.5 36.4 %all-to-all-start.1 = ((bf16[4,264,512]{2,1,0:T(8,128)(2,1)}), bf16[4,264,512]{2,1,0:T(8,128)(2,1)S(1)}, u32[]{:S(2)}, u32[]{:S(2)}) async-start(bf16[4,264,512]{2,1,0:T(8,128)(2,1)} %tile_second.1), calls=%async_computation.1 | async-start | bytes 2162688 | tf_op jit(solution)/shard_map/all_to_all | solution.py:294
  78.5 21.3 %collective-permute-start.4 = (bf16[264,640]{1,0:T(8,128)(2,1)S(1)}, bf16[264,640]{1,0:T(8,128)(2,1)S(1)}, u32[]{:S(2)}, u32[]{:S(2)}) collective-permute-start(bf16[264,640]{1,0:T(8,128)(2,1)S(1)} %get-tuple-element.32), channel_id=1, source_target_pairs={{0,2},{1,3},{2,0},{3,1},{4,6},{5,7},{6,4},{7,5},{8,10},{9,11},{10,... | collective-permute-start | bytes 1013768 | tf_op jit(solution)/shard_map/ppermute | solution.py:267
  83.4 22.1 %collective-permute-start.2 = (bf16[264,640]{1,0:T(8,128)(2,1)S(1)}, bf16[264,640]{1,0:T(8,128)(2,1)S(1)}, u32[]{:S(2)}, u32[]{:S(2)}) collective-permute-start(bf16[264,640]{1,0:T(8,128)(2,1)S(1)} %get-tuple-element.30), channel_id=1, source_target_pairs={{0,1},{1,0},{2,3},{3,2},{4,5},{5,4},{6,7},{7,6},{8,9},{9,8},{10,11... | collective-permute-start | bytes 1013768 | tf_op jit(solution)/shard_map/ppermute | solution.py:275
  85.6 23.3 %collective-permute-start.3 = (bf16[264,640]{1,0:T(8,128)(2,1)S(1)}, bf16[264,640]{1,0:T(8,128)(2,1)S(1)}, u32[]{:S(2)}, u32[]{:S(2)}) collective-permute-start(bf16[264,640]{1,0:T(8,128)(2,1)S(1)} %get-tuple-element.31), channel_id=1, source_target_pairs={{0,3},{1,2},{2,1},{3,0},{4,7},{5,6},{6,5},{7,4},{8,11},{9,10},{10,... | collective-permute-start | bytes 1013768 | tf_op jit(solution)/shard_map/ppermute | solution.py:276
